TPU v7x, 32 devices: a whole 2x2x4 slice. The times are simulated.
32 devices in a mesh: dom: 4 (over y, x), sep: 8 (over z, core).
Axes of the slice: x: 2, y: 2, z: 4, core: 2. Of those that a mesh axis runs over, the one named last changes fastest.
Arguments:
- rhs_leaf: bfloat16 [4, 4096, 1536], P('dom', 'sep'), may hold values from -6 to 6
- rhs_middle: bfloat16 [4, 4096, 768], P('dom', 'sep'), may hold values from -6 to 6
- rhs_top: bfloat16 [4, 4096, 384], P('dom', 'sep'), may hold values from -6 to 6
- update_leaf: bfloat16 [4, 4096, 256], P('dom', 'sep'), may hold values from -0.375 to 0.375
- couple_leaf: bfloat16 [4, 4096, 256], P('dom', 'sep'), may hold values from -0.09375 to 0.09375
- update_middle: bfloat16 [4, 4096, 256], P('dom', 'sep'), may hold values from -0.375 to 0.375, as said below
- couple_middle: bfloat16 [4, 4096, 256], P('dom', 'sep'), may hold values from -0.09375 to 0.09375, as said below
- pivot_leaf: float32 [4, 4096], P('dom', 'sep'), may hold values from 2.2 to 4
- pivot_middle: float32 [2, 4096], P(None, 'sep'), may hold values from 2.2 to 4
- pivot_top: float32 [1, 4096], P(None, 'sep'), may hold values from 2.2 to 4
- front_rows: int32 [4, 8], P('dom', 'sep'), may hold values from 128 to 512, as said below
- rank_leaf: int32 [4], P('dom'), may hold values from 64 to 256, as said below
- rank_middle: int32 [2], replicated, may hold values from 64 to 256, as said below
Outputs:
- top_values: float32 [4, 4096, 384], P('dom', 'sep')
Inputs may be any that keep to these rules, and one draw needn't show every extreme that they name: `front_rows`: in every draw some front has all 512 rows of some row block live. `rank_leaf`: some leaf front has rank 256 in every draw. `rank_middle`: some middle front has rank 256 in every draw. `update_middle`: rows 2g and 2g+1 are equal; entries lie within plus or minus 6 / sqrt(256). `couple_middle`: rows 2g and 2g+1 are equal; entries lie within plus or minus 6 / sqrt(4096).
All inputs are finite; a program needn't handle non-finite values.
Results may differ from a plain program's by a relative error of at most 0.0018.
Values may be sent and summed in bfloat16 or wider, within the bound.
A program may use at most 64 MiB of HBM per device.

v0:
```python
import jax
import jax.numpy as jnp
from jax import lax
from jax.sharding import PartitionSpec as P


def extended(cells, sides, width):
    for axis, dim in sides:
        count = lax.axis_size(axis)
        ends = count - 1
        head = lax.slice_in_dim(cells, 0, width, axis=dim)
        tail = lax.slice_in_dim(cells, cells.shape[dim] - width, cells.shape[dim], axis=dim)
        cells = jnp.concatenate(
            [
                lax.ppermute(tail, axis, [(i, (i + 1) % count) for i in range(ends)]),
                cells,
                lax.ppermute(head, axis, [((i + 1) % count, i) for i in range(ends)]),
            ],
            axis=dim,
        )
    return cells


def from_partner(value, axis, bit):
    mask = 2**bit
    pairs = [(source, source ^ mask) for source in range(lax.axis_size(axis))]
    return lax.ppermute(value, axis, pairs)


def solve_rows(right_side, pivots, row_mask):
    scaled = row_mask[:, None] * right_side / pivots[:, None]
    padded = extended(scaled, (("sep", 0),), 1)
    beside = padded[:-2] + padded[2:]
    return scaled + row_mask[:, None] * beside / pivots[:, None]


def coefficients(factor, values, rank):
    partial_sum = lax.dot_general(
        factor, values, (((0,), (0,)), ((), ())), preferred_element_type=jnp.float32
    )
    rank_keep = (jnp.arange(factor.shape[1]) < rank).astype(jnp.float32)
    kept_sum = partial_sum * rank_keep[:, None]
    return lax.psum(kept_sum, "sep").astype(jnp.bfloat16)


def combine(factor, coef_block, keep_half, swap_bit):
    half_width = coef_block.shape[1] // 2
    own_half = lax.dynamic_slice_in_dim(coef_block, keep_half * half_width, half_width, 1)
    other_half = lax.dynamic_slice_in_dim(coef_block, (1 - keep_half) * half_width, half_width, 1)
    mine_term = jnp.dot(factor, own_half, preferred_element_type=jnp.float32)
    outgoing = jnp.dot(factor, other_half, preferred_element_type=jnp.float32)
    return mine_term + from_partner(outgoing, "dom", swap_bit)


def shards(
    rhs_leaf,
    rhs_middle,
    rhs_top,
    update_leaf,
    couple_leaf,
    update_middle,
    couple_middle,
    pivot_leaf,
    pivot_middle,
    pivot_top,
    front_rows,
    rank_leaf,
    rank_middle,
):
    front = lax.axis_index("dom")
    middle = front // 2
    top_front = front // 4
    row_count = rhs_leaf.shape[1]
    live = (jnp.arange(row_count) < front_rows[0, 0]).astype(jnp.float32)
    every_row = jnp.ones((row_count,), jnp.float32)
    leaf_values = solve_rows(rhs_leaf[0].astype(jnp.float32), pivot_leaf[0], live).astype(
        jnp.bfloat16
    )
    leaf_coef = coefficients(couple_leaf[0], leaf_values, rank_leaf[0])
    middle_rhs = rhs_middle[0].astype(jnp.float32) - combine(
        update_leaf[0], leaf_coef, front % 2, 0
    )
    middle_pivot = lax.dynamic_index_in_dim(pivot_middle, middle, 0, keepdims=False)
    middle_values = solve_rows(middle_rhs, middle_pivot, every_row).astype(jnp.bfloat16)
    middle_rank = lax.dynamic_index_in_dim(rank_middle, middle, 0, keepdims=False)
    middle_coef = coefficients(couple_middle[0], middle_values, middle_rank)
    top_rhs = rhs_top[0].astype(jnp.float32) - combine(update_middle[0], middle_coef, middle % 2, 1)
    top_pivot = lax.dynamic_index_in_dim(pivot_top, top_front, 0, keepdims=False)
    return solve_rows(top_rhs, top_pivot, every_row)[None]


def solution(mesh):
    return jax.shard_map(
        shards,
        mesh=mesh,
        in_specs=(
            P("dom", "sep", None),
            P("dom", "sep", None),
            P("dom", "sep", None),
            P("dom", "sep", None),
            P("dom", "sep", None),
            P("dom", "sep", None),
            P("dom", "sep", None),
            P("dom", "sep"),
            P(None, "sep"),
            P(None, "sep"),
            P("dom", "sep"),
            P("dom"),
            P(),
        ),
        out_specs=P("dom", "sep", None),
        check_vma=False,
    )
```

profile of v0, /device:TPU:24, one launch (start us, length us, event | category | flops | bytes accessed | tf_op | source)
XLA Modules:
  0.0 179.6 jit_solution(2106468252717800136)
XLA Ops:
  0.7 1.8 fusion.4
  2.5 1.9 %collective-permute-start.1 = (f32[1,1536]{1,0:T(1,128)S(1)}, f32[1,1536]{1,0:T(1,128)S(1)}, u32[]{:S(2)}, u32[]{:S(2)}) collective-permute-start(f32[1,1536]{1,0:T(1,128)S(1)} %get-tuple-element.6), channel_id=1, source_target_pairs={{1,0},{2,1},{3,2},{4,3},{5,4},{6,5},{7,6},{9,8},{10,9},{11,10},{12... | collective-permute-start | bytes 18440 | tf_op jit(solution)/shard_map/ppermute | solution.py:17
  4.5 2.4 %collective-permute-start = (f32[1,1536]{1,0:T(1,128)S(1)}, f32[1,1536]{1,0:T(1,128)S(1)}, u32[]{:S(2)}, u32[]{:S(2)}) collective-permute-start(f32[1,1536]{1,0:T(1,128)S(1)} %get-tuple-element.5), channel_id=1, source_target_pairs={{0,1},{1,2},{2,3},{3,4},{4,5},{5,6},{6,7},{8,9},{9,10},{10,11},{11... | collective-permute-start | bytes 18440 | tf_op jit(solution)/shard_map/ppermute | solution.py:15
  7.6 1.8 %collective-permute-done = f32[1,1536]{1,0:T(1,128)S(1)} collective-permute-done((f32[1,1536]{1,0:T(1,128)S(1)}, f32[1,1536]{1,0:T(1,128)S(1)}, u32[]{:S(2)}, u32[]{:S(2)}) %collective-permute-start) | collective-permute-done | bytes 6176 | tf_op jit(solution)/shard_map/ppermute | solution.py:15
  9.4 3.4 %fusion.6 = f32[256,1536]{0,1:T(8,128)} fusion(f32[512,1536]{1,0:T(8,128)S(1)} %fusion.4, f32[1,1536]{1,0:T(1,128)S(1)} %collective-permute-done.1, f32[1,1536]{1,0:T(1,128)S(1)} %collective-permute-done, f32[512]{0:T(512)S(1)} %bitcast.56, f32[512]{0:T(512)S(1)} %fusion.32, f32[256]{0:T(256)S(1)} %compare_convert_fusion.1, bf16[1,512,256]{2,1,0:T(8,128)(2,1)} %param.17), kind=kOutput, calls=%fused_computation.10 | convolution fusion | flops 408551424 | bytes 4998144 | tf_op jit(solution)/shard_map/dot_general | solution.py:38
  12.8 55.7 %all-reduce.2 = bf16[256,1536]{0,1:T(8,128)(2,1)S(1)} all-reduce(f32[256,1536]{0,1:T(8,128)} %fusion.6), channel_id=1, replica_groups=mesh['dom'=4,'sep'=8] {'sep'}, use_global_device_ids=true, to_apply=%region_0.1 | all-reduce | flops 393216 | bytes 2359296 | tf_op jit(solution)/shard_map/psum | solution.py:43
  69.0 1.5 collective-permute-start.2
  70.6 0.6 dynamic_slice.25
  71.2 33.9 %collective-permute-done.2 = f32[512,768]{1,0:T(8,128)} collective-permute-done((f32[512,768]{1,0:T(8,128)S(1)}, f32[512,768]{1,0:T(8,128)}, u32[]{:S(2)}, u32[]{:S(2)}) %collective-permute-start.2) | collective-permute-done | bytes 1572896 | tf_op jit(solution)/shard_map/ppermute | solution.py:27
  105.1 1.8 %fusion.10 = f32[512,768]{1,0:T(8,128)S(1)} fusion(f32[512,768]{1,0:T(8,128)} %collective-permute-done.2, bf16[1,512,768]{2,1,0:T(8,128)(2,1)S(1)} %copy-done.6, f32[512]{0:T(512)S(1)} %bitcast.59, bf16[256,1536]{0,1:T(8,128)(2,1)S(1)} %all-reduce.2, s32[]{:T(128)S(6)} %select_n.37, bf16[1,512,256]{2,1,0:T(8,128)(2,1)S(1)} %copy-done), kind=kOutput, calls=%fused_computation.17 | convolution fusion | flops 202899456 | bytes 4589572 | tf_op jit(solution)/shard_map/dot_general | solution.py:50
  107.0 1.9 %collective-permute-start.4 = (f32[1,768]{1,0:T(1,128)S(1)}, f32[1,768]{1,0:T(1,128)S(1)}, u32[]{:S(2)}, u32[]{:S(2)}) collective-permute-start(f32[1,768]{1,0:T(1,128)S(1)} %get-tuple-element.8), channel_id=1, source_target_pairs={{1,0},{2,1},{3,2},{4,3},{5,4},{6,5},{7,6},{9,8},{10,9},{11,10},{12... | collective-permute-start | bytes 9224 | tf_op jit(solution)/shard_map/ppermute | solution.py:17
  108.9 2.5 %collective-permute-start.3 = (f32[1,768]{1,0:T(1,128)S(1)}, f32[1,768]{1,0:T(1,128)S(1)}, u32[]{:S(2)}, u32[]{:S(2)}) collective-permute-start(f32[1,768]{1,0:T(1,128)S(1)} %get-tuple-element.7), channel_id=1, source_target_pairs={{0,1},{1,2},{2,3},{3,4},{4,5},{5,6},{6,7},{8,9},{9,10},{10,11},{11... | collective-permute-start | bytes 9224 | tf_op jit(solution)/shard_map/ppermute | solution.py:15
  111.4 0.7 compare_convert_fusion
  112.1 1.7 collective-permute-done.3
  113.8 1.6 fusion.16
  115.4 32.5 %all-reduce.3 = bf16[256,768]{0,1:T(8,128)(2,1)S(1)} all-reduce(f32[256,768]{0,1:T(8,128)S(1)} %fusion.16), channel_id=1, replica_groups=mesh['dom'=4,'sep'=8] {'sep'}, use_global_device_ids=true, to_apply=%region_1.2 | all-reduce | flops 196608 | bytes 1179648 | tf_op jit(solution)/shard_map/psum | solution.py:43
  148.3 1.6 collective-permute-start.5
  150.1 18.5 %collective-permute-done.5 = f32[512,384]{0,1:T(8,128)S(1)} collective-permute-done((f32[512,384]{0,1:T(8,128)S(1)}, f32[512,384]{0,1:T(8,128)S(1)}, u32[]{:S(2)}, u32[]{:S(2)}) %collective-permute-start.5) | collective-permute-done | bytes 786464 | tf_op jit(solution)/shard_map/ppermute | solution.py:27
  169.0 1.9 %collective-permute-start.7 = (f32[1,384]{0,1:T(8,128)S(1)}, f32[1,384]{0,1:T(8,128)S(1)}, u32[]{:S(2)}, u32[]{:S(2)}) collective-permute-start(f32[1,384]{0,1:T(8,128)S(1)} %get-tuple-element.10), channel_id=1, source_target_pairs={{1,0},{2,1},{3,2},{4,3},{5,4},{6,5},{7,6},{9,8},{10,9},{11,10},{12... | collective-permute-start | bytes 4616 | tf_op jit(solution)/shard_map/ppermute | solution.py:17
  170.9 2.4 %collective-permute-start.6 = (f32[1,384]{0,1:T(8,128)S(1)}, f32[1,384]{0,1:T(8,128)S(1)}, u32[]{:S(2)}, u32[]{:S(2)}) collective-permute-start(f32[1,384]{0,1:T(8,128)S(1)} %get-tuple-element.9), channel_id=1, source_target_pairs={{0,1},{1,2},{2,3},{3,4},{4,5},{5,6},{6,7},{8,9},{9,10},{10,11},{11... | collective-permute-start | bytes 4616 | tf_op jit(solution)/shard_map/ppermute | solution.py:15
  173.3 0.7 collective-permute-done.7
  174.1 3.8 %collective-permute-done.6 = f32[1,384]{0,1:T(8,128)S(1)} collective-permute-done((f32[1,384]{0,1:T(8,128)S(1)}, f32[1,384]{0,1:T(8,128)S(1)}, u32[]{:S(2)}, u32[]{:S(2)}) %collective-permute-start.6) | collective-permute-done | bytes 1568 | tf_op jit(solution)/shard_map/ppermute | solution.py:15
  177.9 0.5 fusion.20
  178.4 1.1 copy.16
  (28 shorter events, 1.4 us)
Async XLA Ops:
  0.0 68.6 %copy-start = (bf16[1,512,256]{2,1,0:T(8,128)(2,1)S(1)}, bf16[1,512,256]{2,1,0:T(8,128)(2,1)}, u32[]{:S(2)}) copy-start(bf16[1,512,256]{2,1,0:T(8,128)(2,1)} %param.16) | copy-start | bytes 786436
  0.7 8.7 %copy-start.3 = (f32[1,512]{1,0:T(1,128)S(1)}, f32[1,512]{1,0:T(1,128)}, u32[]{:S(2)}) copy-start(f32[1,512]{1,0:T(1,128)} %param.20) | copy-start | bytes 6148
  2.5 5.0 %collective-permute-start.1 = (f32[1,1536]{1,0:T(1,128)S(1)}, f32[1,1536]{1,0:T(1,128)S(1)}, u32[]{:S(2)}, u32[]{:S(2)}) collective-permute-start(f32[1,1536]{1,0:T(1,128)S(1)} %get-tuple-element.6), channel_id=1, source_target_pairs={{1,0},{2,1},{3,2},{4,3},{5,4},{6,5},{7,6},{9,8},{10,9},{11,10},{12... | collective-permute-start | bytes 18440 | tf_op jit(solution)/shard_map/ppermute | solution.py:17
  4.5 4.9 %collective-permute-start = (f32[1,1536]{1,0:T(1,128)S(1)}, f32[1,1536]{1,0:T(1,128)S(1)}, u32[]{:S(2)}, u32[]{:S(2)}) collective-permute-start(f32[1,1536]{1,0:T(1,128)S(1)} %get-tuple-element.5), channel_id=1, source_target_pairs={{0,1},{1,2},{2,3},{3,4},{4,5},{5,6},{6,7},{8,9},{9,10},{10,11},{11... | collective-permute-start | bytes 18440 | tf_op jit(solution)/shard_map/ppermute | solution.py:15
  68.6 2.0 %copy-start.7 = (s32[2]{0:T(128)S(1)}, s32[2]{0:T(128)}, u32[]{:S(2)}) copy-start(s32[2]{0:T(128)} %param.25) | copy-start | bytes 28
  68.6 2.6 %copy-start.5 = (f32[2,512]{1,0:T(2,128)S(1)}, f32[2,512]{1,0:T(2,128)}, u32[]{:S(2)}) copy-start(f32[2,512]{1,0:T(2,128)} %param.21) | copy-start | bytes 12292
  68.6 36.5 %copy-start.6 = (bf16[1,512,768]{2,1,0:T(8,128)(2,1)S(1)}, bf16[1,512,768]{2,1,0:T(8,128)(2,1)}, u32[]{:S(2)}) copy-start(bf16[1,512,768]{2,1,0:T(8,128)(2,1)} %param.14) | copy-start | bytes 2359300
  69.0 36.1 %collective-permute-start.2 = (f32[512,768]{1,0:T(8,128)S(1)}, f32[512,768]{1,0:T(8,128)}, u32[]{:S(2)}, u32[]{:S(2)}) collective-permute-start(f32[512,768]{1,0:T(8,128)S(1)} %convolution_bitcast_fusion), channel_id=1, source_target_pairs={{0,8},{8,0},{16,24},{24,16},{1,9},{9,1},{17,25},{25,17},{2,10},{10... | collective-permute-start | bytes 4718600 | tf_op jit(solution)/shard_map/ppermute | solution.py:27
  107.0 5.1 %collective-permute-start.4 = (f32[1,768]{1,0:T(1,128)S(1)}, f32[1,768]{1,0:T(1,128)S(1)}, u32[]{:S(2)}, u32[]{:S(2)}) collective-permute-start(f32[1,768]{1,0:T(1,128)S(1)} %get-tuple-element.8), channel_id=1, source_target_pairs={{1,0},{2,1},{3,2},{4,3},{5,4},{6,5},{7,6},{9,8},{10,9},{11,10},{12... | collective-permute-start | bytes 9224 | tf_op jit(solution)/shard_map/ppermute | solution.py:17
  108.9 4.9 %collective-permute-start.3 = (f32[1,768]{1,0:T(1,128)S(1)}, f32[1,768]{1,0:T(1,128)S(1)}, u32[]{:S(2)}, u32[]{:S(2)}) collective-permute-start(f32[1,768]{1,0:T(1,128)S(1)} %get-tuple-element.7), channel_id=1, source_target_pairs={{0,1},{1,2},{2,3},{3,4},{4,5},{5,6},{6,7},{8,9},{9,10},{10,11},{11... | collective-permute-start | bytes 9224 | tf_op jit(solution)/shard_map/ppermute | solution.py:15
  112.1 35.9 %copy-start.2 = (bf16[1,512,256]{2,1,0:T(8,128)(2,1)S(1)}, bf16[1,512,256]{2,1,0:T(8,128)(2,1)}, u32[]{:S(2)}) copy-start(bf16[1,512,256]{2,1,0:T(8,128)(2,1)} %param.18) | copy-start | bytes 786436
  115.4 34.4 %copy-start.1 = (bf16[1,512,384]{2,1,0:T(8,128)(2,1)S(1)}, bf16[1,512,384]{2,1,0:T(8,128)(2,1)}, u32[]{:S(2)}) copy-start(bf16[1,512,384]{2,1,0:T(8,128)(2,1)} %param.15) | copy-start | bytes 1179652
  115.4 53.1 %copy-start.4 = (f32[1,512]{1,0:T(1,128)S(1)}, f32[1,512]{1,0:T(1,128)}, u32[]{:S(2)}) copy-start(f32[1,512]{1,0:T(1,128)} %param.22) | copy-start | bytes 6148
  148.3 20.3 %collective-permute-start.5 = (f32[512,384]{0,1:T(8,128)S(1)}, f32[512,384]{0,1:T(8,128)S(1)}, u32[]{:S(2)}, u32[]{:S(2)}) collective-permute-start(f32[512,384]{0,1:T(8,128)S(1)} %convolution_bitcast_fusion.1), channel_id=1, source_target_pairs={{0,16},{8,24},{16,0},{24,8},{1,17},{9,25},{17,1},{25,9},{2,18},{10... | collective-permute-start | bytes 2359304 | tf_op jit(solution)/shard_map/ppermute | solution.py:27
  169.0 5.1 %collective-permute-start.7 = (f32[1,384]{0,1:T(8,128)S(1)}, f32[1,384]{0,1:T(8,128)S(1)}, u32[]{:S(2)}, u32[]{:S(2)}) collective-permute-start(f32[1,384]{0,1:T(8,128)S(1)} %get-tuple-element.10), channel_id=1, source_target_pairs={{1,0},{2,1},{3,2},{4,3},{5,4},{6,5},{7,6},{9,8},{10,9},{11,10},{12... | collective-permute-start | bytes 4616 | tf_op jit(solution)/shard_map/ppermute | solution.py:17
  170.9 7.0 %collective-permute-start.6 = (f32[1,384]{0,1:T(8,128)S(1)}, f32[1,384]{0,1:T(8,128)S(1)}, u32[]{:S(2)}, u32[]{:S(2)}) collective-permute-start(f32[1,384]{0,1:T(8,128)S(1)} %get-tuple-element.9), channel_id=1, source_target_pairs={{0,1},{1,2},{2,3},{3,4},{4,5},{5,6},{6,7},{8,9},{9,10},{10,11},{11... | collective-permute-start | bytes 4616 | tf_op jit(solution)/shard_map/ppermute | solution.py:15
where the time goes:
time: 180 us
  blocking collectives  88.3 us (49%)
  waiting for transfers between devices  60.5 us (34%)
  starting transfers between devices  16.2 us (9%)
  matrix products  7.86 us (4%)
  other arithmetic  2.98 us (2%)
  local copies, waits for them, and re-layouts  2.12 us (1%)
    psum x2, blocking collectives, coefficients(): return lax.psum(kept_sum, 'sep').astype(jnp.bfloat16)  88.3 us
    ppermute x2, waiting for transfers between devices, from_partner(): return lax.ppermute(value, axis, pairs)  52.4 us
    ppermute x3, waiting for transfers between devices, extended(): lax.ppermute(tail, axis, [(i, (i + 1) % count) for i in range(ends)])  7.39 us
    ppermute x3, starting transfers between devices, extended(): lax.ppermute(tail, axis, [(i, (i + 1) % count) for i in range(ends)])  7.3 us
    ppermute x3, starting transfers between devices, extended(): lax.ppermute(head, axis, [((i + 1) % count, i) for i in range(ends)])  5.76 us
    dot_general x2, matrix products, coefficients(): lax.dot_general(factor, values, (((0,), (0,)), ((), ())), preferred_eleme...  5.01 us
  transfers between devices with their start and end apart: 8, of which 6 were waited for; matrix products, arithmetic and copies ran while one was open for 1% of the time, Pallas kernels for 0%

commit v1 on v0

--- a/solution.py
+++ b/solution.py
@@ -40,7 +40,7 @@
     )
     rank_keep = (jnp.arange(factor.shape[1]) < rank).astype(jnp.float32)
     kept_sum = partial_sum * rank_keep[:, None]
-    return lax.psum(kept_sum, "sep").astype(jnp.bfloat16)
+    return jnp.sum(lax.all_gather(kept_sum, "sep"), axis=0).astype(jnp.bfloat16)
 
 
 def combine(factor, coef_block, keep_half, swap_bit):

time: 180 us -> 318 us (1.77)
  waiting for transfers between devices: 60.5 us -> 239 us
  blocking collectives: 88.3 us -> 0 us
  local copies, waits for them, and re-layouts: 2.12 us -> 23.3 us
  between operations: 1.65 us -> 15.1 us
  other arithmetic: 2.98 us -> 13.8 us
    all_gather x0 -> x2, waiting for transfers between devices: none -> 178 us  [coefficients(): return jnp.sum(lax.all_gather(kept_sum, 'sep'), axis=0).astype(jnp.bfloat16)]
    psum x2 -> x0, blocking collectives: 88.3 us -> none  [coefficients(): return lax.psum(kept_sum, 'sep').astype(jnp.bfloat16)]
    unnamed x17 -> x23, local copies, waits for them, and re-layouts: 0.25 us -> 21.4 us
    reduce_sum x0 -> x2, other arithmetic: none -> 10.8 us  [coefficients(): return jnp.sum(lax.all_gather(kept_sum, 'sep'), axis=0).astype(jnp.bfloat16)]
  transfers between devices with their start and end apart: 8 -> 10, of which waited for: 6 -> 8; matrix products, arithmetic and copies ran while one was open for 1% -> 0% of each run, Pallas kernels for 0% -> 0%
where the time goes in v1:
time: 318 us; the launch traced here: 315 us
  waiting for transfers between devices  239 us (75%)
  local copies, waits for them, and re-layouts  23.3 us (7%)
  starting transfers between devices  17.2 us (5%)
  between operations  15.1 us (5%)
  other arithmetic  13.8 us (4%)
  matrix products  6.88 us (2%)
    all_gather x2, waiting for transfers between devices, coefficients(): return jnp.sum(lax.all_gather(kept_sum, 'sep'), axis=0).astype(jnp.bfloat16)  178 us
    ppermute x2, waiting for transfers between devices, from_partner(): return lax.ppermute(value, axis, pairs)  52.2 us
    unnamed x23, local copies, waits for them, and re-layouts  21.4 us
    reduce_sum x2, other arithmetic, coefficients(): return jnp.sum(lax.all_gather(kept_sum, 'sep'), axis=0).astype(jnp.bfloat16)  10.8 us
    ppermute x3, waiting for transfers between devices, extended(): lax.ppermute(tail, axis, [(i, (i + 1) % count) for i in range(ends)])  7.83 us
    ppermute x3, starting transfers between devices, extended(): lax.ppermute(head, axis, [((i + 1) % count, i) for i in range(ends)])  7.29 us
    ppermute x3, starting transfers between devices, extended(): lax.ppermute(tail, axis, [(i, (i + 1) % count) for i in range(ends)])  6.42 us
  transfers between devices with their start and end apart: 10, of which 8 were waited for; matrix products, arithmetic and copies ran while one was open for 0% of the time, Pallas kernels for 0%

profile of v1, /device:TPU:24, one launch (start us, length us, event | category | flops | bytes accessed | tf_op | source)
XLA Modules:
  0.0 315.4 jit_solution(4612154368937314650)
XLA Ops:
  7.3 1.8 fusion.4
  9.1 1.9 collective-permute-start.1
  11.1 2.4 collective-permute-start
  14.1 1.9 collective-permute-done
  16.0 2.5 fusion.6
  18.6 114.7 %all-gather.5.cloned.1.call-done = f32[2048,1536]{0,1:T(8,128)} async-done(((f32[256,1536]{0,1:T(8,128)}), f32[2048,1536]{0,1:T(8,128)}) %all-gather.5.cloned.1.call-update) | async-done | bytes 12582928 | tf_op jit(solution)/shard_map/all_gather | solution.py:43
  133.3 15.3 %copy.21 = f32[192,8,8,256]{3,2,1,0:T(8,128)} copy(f32[192,8,8,256]{3,1,2,0:T(8,128)} %bitcast.65) | data formatting | bytes 25165824
  148.7 8.9 %bitcast_reduce_fusion = bf16[256,1536]{0,1:T(8,128)(2,1)S(1)} fusion(f32[192,8,8,256]{3,2,1,0:T(8,128)} %copy.21), kind=kLoop, calls=%fused_computation | loop fusion | flops 2752512 | bytes 13369344 | tf_op jit(solution)/shard_map/reduce_sum | solution.py:43
  158.0 1.7 collective-permute-start.2
  160.3 34.4 %collective-permute-done.2 = f32[512,768]{1,0:T(8,128)} collective-permute-done((f32[512,768]{1,0:T(8,128)S(1)}, f32[512,768]{1,0:T(8,128)}, u32[]{:S(2)}, u32[]{:S(2)}) %collective-permute-start.2) | collective-permute-done | bytes 1572896 | tf_op jit(solution)/shard_map/ppermute | solution.py:27
  194.7 1.9 fusion.10
  196.6 2.7 collective-permute-start.4
  199.3 2.1 collective-permute-start.3
  202.1 2.1 collective-permute-done.3
  204.2 1.5 fusion.16
  205.8 63.1 %all-gather.7.cloned.1.call-done = f32[2048,768]{0,1:T(8,128)} async-done(((f32[256,768]{0,1:T(8,128)}), f32[2048,768]{0,1:T(8,128)}) %all-gather.7.cloned.1.call-update) | async-done | bytes 6291472 | tf_op jit(solution)/shard_map/all_gather | solution.py:43
  268.9 5.8 %copy.22 = f32[96,8,8,256]{3,2,1,0:T(8,128)S(1)} copy(f32[96,8,8,256]{3,1,2,0:T(8,128)} %bitcast.66) | data formatting | bytes 12582912
  274.8 2.0 bitcast_reduce_fusion.1
  277.0 1.7 collective-permute-start.5
  279.0 17.8 %collective-permute-done.5 = f32[512,384]{0,1:T(8,128)S(1)} collective-permute-done((f32[512,384]{0,1:T(8,128)S(1)}, f32[512,384]{0,1:T(8,128)S(1)}, u32[]{:S(2)}, u32[]{:S(2)}) %collective-permute-start.5) | collective-permute-done | bytes 786464 | tf_op jit(solution)/shard_map/ppermute | solution.py:27
  297.2 2.7 collective-permute-start.7
  299.9 1.9 collective-permute-start.6
  301.8 1.2 collective-permute-done.7
  303.1 3.8 %collective-permute-done.6 = f32[1,384]{0,1:T(8,128)S(1)} collective-permute-done((f32[1,384]{0,1:T(8,128)S(1)}, f32[1,384]{0,1:T(8,128)S(1)}, u32[]{:S(2)}, u32[]{:S(2)}) %collective-permute-start.6) | collective-permute-done | bytes 1568 | tf_op jit(solution)/shard_map/ppermute | solution.py:15
  (40 shorter events, 4.4 us)
Async XLA Ops:
  6.5 151.0 %copy-start = (bf16[1,512,256]{2,1,0:T(8,128)(2,1)S(1)}, bf16[1,512,256]{2,1,0:T(8,128)(2,1)}, u32[]{:S(2)}) copy-start(bf16[1,512,256]{2,1,0:T(8,128)(2,1)} %param.16) | copy-start | bytes 786436
  6.5 126.8 %all-gather.5.cloned.1.call-start = ((), (), s32[]{:S(2)}) async-start(), calls=%async_computation | async-start | bytes 14155776 | tf_op jit(solution)/shard_map/all_gather | solution.py:43
  7.2 8.8 %copy-start.3 = (f32[1,512]{1,0:T(1,128)S(1)}, f32[1,512]{1,0:T(1,128)}, u32[]{:S(2)}) copy-start(f32[1,512]{1,0:T(1,128)} %param.20) | copy-start | bytes 6148
  7.3 8.8 %copy-start.7 = (bf16[1,512,256]{2,1,0:T(8,128)(2,1)S(1)}, bf16[1,512,256]{2,1,0:T(8,128)(2,1)}, u32[]{:S(2)}) copy-start(bf16[1,512,256]{2,1,0:T(8,128)(2,1)} %param.17) | copy-start | bytes 786436
  9.1 5.0 %collective-permute-start.1 = (f32[1,1536]{1,0:T(1,128)S(1)}, f32[1,1536]{1,0:T(1,128)S(1)}, u32[]{:S(2)}, u32[]{:S(2)}) collective-permute-start(f32[1,1536]{1,0:T(1,128)S(1)} %get-tuple-element.6), channel_id=1, source_target_pairs={{1,0},{2,1},{3,2},{4,3},{5,4},{6,5},{7,6},{9,8},{10,9},{11,10},{12... | collective-permute-start | bytes 18440 | tf_op jit(solution)/shard_map/ppermute | solution.py:17
  11.1 4.9 %collective-permute-start = (f32[1,1536]{1,0:T(1,128)S(1)}, f32[1,1536]{1,0:T(1,128)S(1)}, u32[]{:S(2)}, u32[]{:S(2)}) collective-permute-start(f32[1,1536]{1,0:T(1,128)S(1)} %get-tuple-element.5), channel_id=1, source_target_pairs={{0,1},{1,2},{2,3},{3,4},{4,5},{5,6},{6,7},{8,9},{9,10},{10,11},{11... | collective-permute-start | bytes 18440 | tf_op jit(solution)/shard_map/ppermute | solution.py:15
  18.5 250.4 %all-gather.7.cloned.1.call-start = ((), (), s32[]{:S(2)}) async-start(), calls=%async_computation.1 | async-start | bytes 7077888 | tf_op jit(solution)/shard_map/all_gather | solution.py:43
  157.5 2.2 copy-start.9
  157.6 2.8 copy-start.5
  157.6 37.1 %copy-start.6 = (bf16[1,512,768]{2,1,0:T(8,128)(2,1)S(1)}, bf16[1,512,768]{2,1,0:T(8,128)(2,1)}, u32[]{:S(2)}) copy-start(bf16[1,512,768]{2,1,0:T(8,128)(2,1)} %param.14) | copy-start | bytes 2359300
  158.0 36.7 %collective-permute-start.2 = (f32[512,768]{1,0:T(8,128)S(1)}, f32[512,768]{1,0:T(8,128)}, u32[]{:S(2)}, u32[]{:S(2)}) collective-permute-start(f32[512,768]{1,0:T(8,128)S(1)} %convolution_bitcast_fusion), channel_id=1, source_target_pairs={{0,8},{8,0},{16,24},{24,16},{1,9},{9,1},{17,25},{25,17},{2,10},{10... | collective-permute-start | bytes 4718600 | tf_op jit(solution)/shard_map/ppermute | solution.py:27
  194.7 9.5 %copy-start.8 = (bf16[1,512,256]{2,1,0:T(8,128)(2,1)S(1)}, bf16[1,512,256]{2,1,0:T(8,128)(2,1)}, u32[]{:S(2)}) copy-start(bf16[1,512,256]{2,1,0:T(8,128)(2,1)} %param.19) | copy-start | bytes 786436
  196.6 5.5 %collective-permute-start.4 = (f32[1,768]{1,0:T(1,128)S(1)}, f32[1,768]{1,0:T(1,128)S(1)}, u32[]{:S(2)}, u32[]{:S(2)}) collective-permute-start(f32[1,768]{1,0:T(1,128)S(1)} %get-tuple-element.8), channel_id=1, source_target_pairs={{1,0},{2,1},{3,2},{4,3},{5,4},{6,5},{7,6},{9,8},{10,9},{11,10},{12... | collective-permute-start | bytes 9224 | tf_op jit(solution)/shard_map/ppermute | solution.py:17
  199.3 4.9 %collective-permute-start.3 = (f32[1,768]{1,0:T(1,128)S(1)}, f32[1,768]{1,0:T(1,128)S(1)}, u32[]{:S(2)}, u32[]{:S(2)}) collective-permute-start(f32[1,768]{1,0:T(1,128)S(1)} %get-tuple-element.7), channel_id=1, source_target_pairs={{0,1},{1,2},{2,3},{3,4},{4,5},{5,6},{6,7},{8,9},{9,10},{10,11},{11... | collective-permute-start | bytes 9224 | tf_op jit(solution)/shard_map/ppermute | solution.py:15
  274.7 2.0 copy-start.2
  274.8 4.0 %copy-start.1 = (bf16[1,512,384]{2,1,0:T(8,128)(2,1)S(1)}, bf16[1,512,384]{2,1,0:T(8,128)(2,1)}, u32[]{:S(2)}) copy-start(bf16[1,512,384]{2,1,0:T(8,128)(2,1)} %param.15) | copy-start | bytes 1179652
  276.7 20.1 %copy-start.4 = (f32[1,512]{1,0:T(1,128)S(1)}, f32[1,512]{1,0:T(1,128)}, u32[]{:S(2)}) copy-start(f32[1,512]{1,0:T(1,128)} %param.22) | copy-start | bytes 6148
  277.0 19.7 %collective-permute-start.5 = (f32[512,384]{0,1:T(8,128)S(1)}, f32[512,384]{0,1:T(8,128)S(1)}, u32[]{:S(2)}, u32[]{:S(2)}) collective-permute-start(f32[512,384]{0,1:T(8,128)S(1)} %convolution_bitcast_fusion.1), channel_id=1, source_target_pairs={{0,16},{8,24},{16,0},{24,8},{1,17},{9,25},{17,1},{25,9},{2,18},{10... | collective-permute-start | bytes 2359304 | tf_op jit(solution)/shard_map/ppermute | solution.py:27
  297.2 5.9 %collective-permute-start.7 = (f32[1,384]{0,1:T(8,128)S(1)}, f32[1,384]{0,1:T(8,128)S(1)}, u32[]{:S(2)}, u32[]{:S(2)}) collective-permute-start(f32[1,384]{0,1:T(8,128)S(1)} %get-tuple-element.10), channel_id=1, source_target_pairs={{1,0},{2,1},{3,2},{4,3},{5,4},{6,5},{7,6},{9,8},{10,9},{11,10},{12... | collective-permute-start | bytes 4616 | tf_op jit(solution)/shard_map/ppermute | solution.py:17
  299.9 7.0 %collective-permute-start.6 = (f32[1,384]{0,1:T(8,128)S(1)}, f32[1,384]{0,1:T(8,128)S(1)}, u32[]{:S(2)}, u32[]{:S(2)}) collective-permute-start(f32[1,384]{0,1:T(8,128)S(1)} %get-tuple-element.9), channel_id=1, source_target_pairs={{0,1},{1,2},{2,3},{3,4},{4,5},{5,6},{6,7},{8,9},{9,10},{10,11},{11... | collective-permute-start | bytes 4616 | tf_op jit(solution)/shard_map/ppermute | solution.py:15
Sparse Core Ops, SparseCore 0:
  18.7 114.6 all-gather.4
  205.9 62.9 all-gather.6
